TPU v7x, 32 devices: a whole 2x2x4 slice. The times are simulated.
32 devices in a mesh: expert: 8 (over z, x), tensor: 4 (over y, core).
Axes of the slice: x: 2, y: 2, z: 4, core: 2. Of those that a mesh axis runs over, the one named last changes fastest.
Arguments:
- tokens: bfloat16 [512, 8192], P('expert', 'tensor'), may hold values from -6 to 6
- frozen_gate_weight: bfloat16 [8192, 28672], P('tensor', 'expert'), may hold values from -0.0625 to 0.0625
- frozen_up_weight: bfloat16 [8192, 28672], P('tensor', 'expert'), may hold values from -0.0625 to 0.0625
- frozen_down_weight: bfloat16 [28672, 8192], P('expert', 'tensor'), may hold values from -0.03125 to 0.03125
- adapter_down_weight: bfloat16 [32, 8192, 128], P('expert', 'tensor'), may hold values from -0.0625 to 0.0625
- adapter_up_weight: bfloat16 [32, 128, 8192], P('expert', None, 'tensor'), may hold values from -0.0625 to 0.0625
- routes: int32 [512, 2], P('expert'), may hold values from 0 to 31, all different within a row; in each aligned block of 64 rows (0 to 63, 64 to 127, ...) at most 8 rows name the same one
- route_gate_weights: float32 [512, 2], P('expert'), may hold values from 0.1 to 1
- output_gradient: bfloat16 [512, 8192], P('expert', 'tensor'), may hold values from -6 to 6
Outputs:
- ffn_out: bfloat16 [512, 8192], P('expert', 'tensor')
- grad_down: bfloat16 [32, 8192, 128], P('expert', 'tensor')
- grad_up: bfloat16 [32, 128, 8192], P('expert', None, 'tensor')
Inputs may be any that keep to these rules, and one draw needn't show every extreme that they name: `routes`: the two experts of a token differ. Among the 64 rows of one index of expert no expert is named more than 8 times, and in some such rows one expert is named exactly 8 times.
All inputs are finite; a program needn't handle non-finite values.
Results may differ from a plain program's by a relative error of at most 0.025.
Values may be sent and summed in bfloat16 or wider, within the bound.
A program may use at most 128 MiB of HBM per device.

v0:
```python
import jax
import jax.numpy as jnp
from jax import lax
from jax.sharding import PartitionSpec as P


def activate(summed, hidden_width):
    gate_part = summed[:, :hidden_width]
    up_part = summed[:, hidden_width:]
    return (jax.nn.silu(gate_part) * up_part).astype(jnp.bfloat16)


def per_device(
    tokens,
    frozen_gate_weight,
    frozen_up_weight,
    frozen_down_weight,
    adapter_down_weight,
    adapter_up_weight,
    routes,
    route_gate_weights,
    output_gradient,
):
    n_expert = lax.axis_size("expert")
    tok_count, width_part = tokens.shape
    hidden_width = frozen_gate_weight.shape[1]
    expert_resident = adapter_down_weight.shape[0]
    all_experts = expert_resident * n_expert
    most_slots = max(2, 4 * tok_count // all_experts)
    slot_total = all_experts * most_slots
    per_peer = expert_resident * most_slots
    shard_rows = lax.all_gather(tokens, "expert", axis=0, tiled=True)
    gate_part = jnp.dot(shard_rows, frozen_gate_weight, preferred_element_type=jnp.float32)
    up_part = jnp.dot(shard_rows, frozen_up_weight, preferred_element_type=jnp.float32)
    partial_value = jnp.concatenate([gate_part, up_part], axis=1)
    summed = lax.psum_scatter(
        partial_value.astype(jnp.bfloat16), "tensor", scatter_dimension=0, tiled=True
    ).astype(jnp.float32)
    hidden_all = lax.all_gather(activate(summed, hidden_width), "tensor", axis=0, tiled=True)
    base_out = lax.psum_scatter(
        jnp.dot(hidden_all, frozen_down_weight, preferred_element_type=jnp.float32).astype(
            jnp.bfloat16
        ),
        "expert",
        scatter_dimension=0,
        tiled=True,
    ).astype(jnp.float32)
    route_ids = routes.reshape(-1)
    pair_count = route_ids.shape[0]
    expert_range = jnp.arange(all_experts, dtype=jnp.int32)
    member = (route_ids[:, None] == expert_range[None, :]).astype(jnp.bfloat16)
    pair_range = jnp.arange(pair_count, dtype=jnp.int32)
    before = (pair_range[:, None] > pair_range[None, :]).astype(jnp.bfloat16)
    earlier = jnp.dot(before, member, preferred_element_type=jnp.float32)
    within = jnp.sum(earlier * member.astype(jnp.float32), axis=1).astype(jnp.int32)
    target = route_ids * most_slots + within
    slot_range = jnp.arange(slot_total, dtype=jnp.int32)
    select = (slot_range[:, None] == target[None, :]).astype(jnp.bfloat16)
    to_slots = jnp.sum(select.reshape(slot_total, tok_count, 2), axis=2)
    send_inputs = jnp.dot(to_slots, tokens, preferred_element_type=jnp.float32).astype(jnp.bfloat16)
    send_inputs = send_inputs.reshape(n_expert, per_peer, width_part)
    scaled = (
        route_gate_weights[:, :, None] * output_gradient[:, None, :].astype(jnp.float32)
    ).astype(jnp.bfloat16)
    scaled = scaled.reshape(pair_count, width_part)
    send_grads = jnp.dot(select, scaled, preferred_element_type=jnp.float32).astype(jnp.bfloat16)
    send_grads = send_grads.reshape(n_expert, per_peer, width_part)
    incoming_input_rows = lax.all_to_all(
        send_inputs, "expert", split_axis=0, concat_axis=0, tiled=True
    )
    incoming_input_rows = incoming_input_rows.reshape(
        n_expert, expert_resident, most_slots, width_part
    )
    low_sum = lax.psum(
        jnp.einsum(
            "bcwk,cko->cbwo",
            incoming_input_rows,
            adapter_down_weight,
            preferred_element_type=jnp.float32,
        ).astype(jnp.bfloat16),
        "tensor",
    )
    expert_out = jnp.einsum(
        "lugx,lxo->ulgo", low_sum, adapter_up_weight, preferred_element_type=jnp.float32
    ).astype(jnp.bfloat16)
    returned = lax.all_to_all(
        expert_out.reshape(n_expert, per_peer, width_part),
        "expert",
        split_axis=0,
        concat_axis=0,
        tiled=True,
    )
    per_pair = jnp.dot(
        select.T, returned.reshape(slot_total, width_part), preferred_element_type=jnp.float32
    )
    per_pair = per_pair.reshape(tok_count, 2, width_part)
    adapter_sum = (
        route_gate_weights[:, 0:1] * per_pair[:, 0, :]
        + route_gate_weights[:, 1:2] * per_pair[:, 1, :]
    )
    ffn_out = (base_out + adapter_sum).astype(jnp.bfloat16)
    incoming_gradients = lax.all_to_all(
        send_grads, "expert", split_axis=0, concat_axis=0, tiled=True
    )
    incoming_gradients = incoming_gradients.reshape(
        n_expert, expert_resident, most_slots, width_part
    )
    back_sum = lax.psum(
        jnp.einsum(
            "nhpf,hxf->hnpx",
            incoming_gradients,
            adapter_up_weight,
            preferred_element_type=jnp.float32,
        ).astype(jnp.bfloat16),
        "tensor",
    )
    grad_up = jnp.einsum(
        "jsmr,sjmd->jrd", low_sum, incoming_gradients, preferred_element_type=jnp.float32
    ).astype(jnp.bfloat16)
    grad_down = jnp.einsum(
        "sjmd,jsmr->jdr", incoming_input_rows, back_sum, preferred_element_type=jnp.float32
    ).astype(jnp.bfloat16)
    return (ffn_out, grad_down, grad_up)


def solution(mesh):
    placed = (
        P("expert", "tensor"),
        P("tensor", "expert"),
        P("tensor", "expert"),
        P("expert", "tensor"),
        P("expert", "tensor", None),
        P("expert", None, "tensor"),
        P("expert", None),
        P("expert", None),
        P("expert", "tensor"),
    )
    return jax.shard_map(
        per_device,
        mesh=mesh,
        in_specs=placed,
        out_specs=(P("expert", "tensor"), P("expert", "tensor", None), P("expert", None, "tensor")),
        check_vma=False,
    )
```

profile of v0, /device:TPU:0, one launch (start us, length us, event | category | flops | bytes accessed | tf_op | source)
XLA Modules:
  0.0 356.5 jit_solution(9830163328550035932)
XLA Ops:
  7.2 0.0 all-gather.3.cloned.1.call-start
  7.2 0.7 all-gather.3.cloned.1.call-update
  7.9 0.0 reduce-scatter.3.cloned.1.call-start
  8.0 54.0 %all-gather.3.cloned.1.call-done = bf16[512,2048]{1,0:T(8,128)(2,1)} async-done(((bf16[64,2048]{1,0:T(8,128)(2,1)}), bf16[512,2048]{1,0:T(8,128)(2,1)}) %all-gather.3.cloned.1.call-update) | async-done | bytes 2097168 | tf_op jit(solution)/shard_map/all_gather | solution.py:32
  62.0 14.9 %convolution_convert_fusion = bf16[512,3584]{1,0:T(8,128)(2,1)} fusion(bf16[512,2048]{1,0:T(8,128)(2,1)} %all-gather.3.cloned.1.call-done, bf16[2048,3584]{1,0:T(8,128)(2,1)} %param.11), kind=kOutput, calls=%fused_computation.1 | convolution fusion | flops 7518027776 | bytes 20447232 | tf_op jit(solution)/shard_map/dot_general | solution.py:34
  76.9 12.4 %convolution_convert_fusion.1 = bf16[512,3584]{1,0:T(8,128)(2,1)} fusion(bf16[512,2048]{1,0:T(8,128)(2,1)S(1)} %copy-done.6, bf16[2048,3584]{1,0:T(8,128)(2,1)} %param.10), kind=kOutput, calls=%fused_computation.2 | convolution fusion | flops 7518027776 | bytes 20447232 | tf_op jit(solution)/shard_map/dot_general | solution.py:33
  89.3 6.9 %pad_maximum_fusion = bf16[512,7168]{1,0:T(8,128)(2,1)} fusion(bf16[512,3584]{1,0:T(8,128)(2,1)} %convolution_convert_fusion, bf16[512,3584]{1,0:T(8,128)(2,1)} %convolution_convert_fusion.1), kind=kLoop, calls=%fused_computation | loop fusion | flops 14680064 | bytes 14680064 | tf_op jit(solution)/shard_map/concatenate | solution.py:35
  96.1 0.0 reduce-scatter.3.cloned.1.call-update
  96.2 0.0 all-gather.5.cloned.1.call-start
  96.2 64.6 %reduce-scatter.3.cloned.1.call-done = bf16[128,7168]{1,0:T(8,128)(2,1)} async-done(((bf16[512,7168]{1,0:T(8,128)(2,1)}), bf16[128,7168]{1,0:T(8,128)(2,1)}) %reduce-scatter.3.cloned.1.call-update) | async-done | bytes 1835024 | tf_op jit(solution)/shard_map/reduce_scatter | solution.py:36
  160.8 1.9 convert_element_type.72
  162.7 1.5 fusion.6
  164.1 0.0 all-gather.5.cloned.1.call-update
  164.2 0.1 copy.40
  164.3 0.1 reshape.81
  164.4 0.5 mul.78
  164.9 1.7 mul.79
  166.6 0.1 copy.45
  166.7 0.1 mul.76
  166.9 0.2 fusion.13
  167.1 2.7 convolution_convert_fusion.3
  169.8 5.5 %all-to-all-start.2 = ((bf16[8,32,2048]{2,1,0:T(8,128)(2,1)}), bf16[8,32,2048]{2,1,0:T(8,128)(2,1)S(1)}, u32[]{:S(2)}, u32[]{:S(2)}) async-start(bf16[8,32,2048]{2,1,0:T(8,128)(2,1)} %bitcast.77), calls=%async_computation.4 | async-start | bytes 2097152 | tf_op jit(solution)/shard_map/all_to_all | solution.py:102
  175.3 0.1 convert_element_type.79
  175.5 0.1 copy.41
  175.5 0.1 fusion.25
  175.7 1.4 convolution_convert_fusion.5
  177.1 23.9 %all-to-all-done.2 = bf16[8,32,2048]{2,1,0:T(8,128)(2,1)S(1)} async-done(((bf16[8,32,2048]{2,1,0:T(8,128)(2,1)}), bf16[8,32,2048]{2,1,0:T(8,128)(2,1)S(1)}, u32[]{:S(2)}, u32[]{:S(2)}) %all-to-all-start.2) | async-done | bytes 1048608 | tf_op jit(solution)/shard_map/all_to_all | solution.py:102
  201.0 4.3 %all-to-all-start = ((bf16[8,32,2048]{2,1,0:T(8,128)(2,1)}), bf16[8,32,2048]{2,1,0:T(8,128)(2,1)}, u32[]{:S(2)}, u32[]{:S(2)}) async-start(bf16[8,32,2048]{2,1,0:T(8,128)(2,1)} %bitcast.76), calls=%async_computation.2 | async-start | bytes 2097152 | tf_op jit(solution)/shard_map/all_to_all | solution.py:68
  205.2 0.0 all-reduce.3.cloned.1.call-start
  205.3 0.6 copy.46
  205.9 1.5 fusion.7
  207.4 23.4 %all-to-all-done = bf16[8,32,2048]{2,1,0:T(8,128)(2,1)} async-done(((bf16[8,32,2048]{2,1,0:T(8,128)(2,1)}), bf16[8,32,2048]{2,1,0:T(8,128)(2,1)}, u32[]{:S(2)}, u32[]{:S(2)}) %all-to-all-start) | async-done | bytes 1048608 | tf_op jit(solution)/shard_map/all_to_all | solution.py:68
  230.8 3.0 fusion.10
  233.8 0.0 all-reduce.3.cloned.1.call-update
  233.8 0.2 reduce-scatter.5.cloned.1.call-start
  234.0 0.0 all-gather.5.cloned.1.call-done
  234.1 13.1 %convolution_convert_fusion.2 = bf16[512,2048]{1,0:T(8,128)(2,1)} fusion(bf16[512,3584]{1,0:T(8,128)(2,1)} %all-gather.5.cloned.1.call-done, bf16[3584,2048]{1,0:T(8,128)(2,1)} %param.12), kind=kOutput, calls=%fused_computation.5 | convolution fusion | flops 7517241344 | bytes 20447232 | tf_op jit(solution)/shard_map/dot_general | solution.py:41
  247.2 16.4 %all-reduce.3.cloned.1.call-done = (bf16[4,8,8,128]{3,2,1,0:T(8,128)(2,1)}, bf16[4,8,8,128]{3,1,2,0:T(8,128)(2,1)}) async-done(((bf16[4,8,8,128]{3,2,1,0:T(8,128)(2,1)}, bf16[4,8,8,128]{3,1,2,0:T(8,128)(2,1)}), (bf16[4,8,8,128]{3,2,1,0:T(8,128)(2,1)}, bf16[4,8,8,128]{3,1,2,0:T(8,128)(2,1)})) %all-reduce.3.cloned.1.call-update) | async-done | bytes 131088 | tf_op jit(solution)/shard_map/psum | solution.py:74
  263.6 1.3 fusion
  264.9 1.1 copy.62
  266.0 5.5 %all-to-all-start.1 = ((bf16[8,32,2048]{2,1,0:T(8,128)(2,1)}), bf16[8,32,2048]{2,1,0:T(8,128)(2,1)}, u32[]{:S(2)}, u32[]{:S(2)}) async-start(bf16[8,32,2048]{2,1,0:T(8,128)(2,1)} %bitcast.75), calls=%async_computation.3 | async-start | bytes 2097152 | tf_op jit(solution)/shard_map/all_to_all | solution.py:86
  271.5 0.1 iota_compare_fusion.2
  271.7 2.1 bitcast_convert_fusion
  273.7 3.5 bitcast_convert_fusion.1
  277.2 36.2 %all-to-all-done.1 = bf16[8,32,2048]{2,1,0:T(8,128)(2,1)} async-done(((bf16[8,32,2048]{2,1,0:T(8,128)(2,1)}), bf16[8,32,2048]{2,1,0:T(8,128)(2,1)}, u32[]{:S(2)}, u32[]{:S(2)}) %all-to-all-start.1) | async-done | bytes 1048608 | tf_op jit(solution)/shard_map/all_to_all | solution.py:86
  313.4 1.5 fusion.23
  314.9 33.2 %reduce-scatter.5.cloned.1.call-done = bf16[64,2048]{1,0:T(8,128)(2,1)} async-done(((bf16[512,2048]{1,0:T(8,128)(2,1)}), bf16[64,2048]{1,0:T(8,128)(2,1)}) %reduce-scatter.5.cloned.1.call-update) | async-done | bytes 262160 | tf_op jit(solution)/shard_map/reduce_scatter | solution.py:40
  348.2 1.8 fusion.19
  (22 shorter events, 0.1 us)
Async XLA Ops:
  7.2 198.7 %copy-start = (bf16[4,128,2048]{2,1,0:T(8,128)(2,1)S(1)}, bf16[4,128,2048]{2,1,0:T(8,128)(2,1)}, u32[]{:S(2)}) copy-start(bf16[4,128,2048]{2,1,0:T(8,128)(2,1)} %param.14) | copy-start | bytes 6291460
  7.2 54.8 %all-gather.3.cloned.1.call-start = ((), (), s32[]{:S(2)}) async-start(), calls=%async_computation.5 | async-start | bytes 2359296 | tf_op jit(solution)/shard_map/all_gather | solution.py:32
  7.9 152.9 %reduce-scatter.3.cloned.1.call-start = ((), (), s32[]{:S(2)}) async-start(), calls=%async_computation.6 | async-start | bytes 9175040 | tf_op jit(solution)/shard_map/reduce_scatter | solution.py:36
  62.0 14.9 %copy-start.6 = (bf16[512,2048]{1,0:T(8,128)(2,1)S(1)}, bf16[512,2048]{1,0:T(8,128)(2,1)}, u32[]{:S(2)}) copy-start(bf16[512,2048]{1,0:T(8,128)(2,1)} %all-gather.3.cloned.1.call-done) | copy-start | bytes 6291460
  96.2 137.9 %all-gather.5.cloned.1.call-start = ((), (), s32[]{:S(2)}) async-start(), calls=%async_computation.7 | async-start | bytes 4587520 | tf_op jit(solution)/shard_map/all_gather | solution.py:39
  162.7 1.5 copy-start.4
  162.7 1.7 copy-start.3
  164.1 2.5 copy-start.5
  167.0 8.6 %copy-start.1 = (bf16[64,2048]{1,0:T(8,128)(2,1)S(1)}, bf16[64,2048]{1,0:T(8,128)(2,1)}, u32[]{:S(2)}) copy-start(bf16[64,2048]{1,0:T(8,128)(2,1)} %param.9) | copy-start | bytes 786436
  169.8 31.2 %all-to-all-start.2 = ((bf16[8,32,2048]{2,1,0:T(8,128)(2,1)}), bf16[8,32,2048]{2,1,0:T(8,128)(2,1)S(1)}, u32[]{:S(2)}, u32[]{:S(2)}) async-start(bf16[8,32,2048]{2,1,0:T(8,128)(2,1)} %bitcast.77), calls=%async_computation.4 | async-start | bytes 2097152 | tf_op jit(solution)/shard_map/all_to_all | solution.py:102
  201.0 29.8 %all-to-all-start = ((bf16[8,32,2048]{2,1,0:T(8,128)(2,1)}), bf16[8,32,2048]{2,1,0:T(8,128)(2,1)}, u32[]{:S(2)}, u32[]{:S(2)}) async-start(bf16[8,32,2048]{2,1,0:T(8,128)(2,1)} %bitcast.76), calls=%async_computation.2 | async-start | bytes 2097152 | tf_op jit(solution)/shard_map/all_to_all | solution.py:68
  205.2 58.4 %all-reduce.3.cloned.1.call-start = ((), (), s32[]{:S(2)}) async-start(), calls=%async_computation.9 | async-start | bytes 262144 | tf_op jit(solution)/shard_map/psum | solution.py:74
  233.8 114.4 %reduce-scatter.5.cloned.1.call-start = ((), (), s32[]{:S(2)}) async-start(), calls=%async_computation.8 | async-start | bytes 2359296 | tf_op jit(solution)/shard_map/reduce_scatter | solution.py:40
  264.9 6.7 %copy-start.2 = (bf16[4,8,8,128]{3,2,1,0:T(8,128)(2,1)S(1)}, bf16[4,8,8,128]{3,2,1,0:T(8,128)(2,1)}, u32[]{:S(2)}) copy-start(bf16[4,8,8,128]{3,2,1,0:T(8,128)(2,1)} %get-tuple-element.3) | copy-start | bytes 196612
  266.0 47.4 %all-to-all-start.1 = ((bf16[8,32,2048]{2,1,0:T(8,128)(2,1)}), bf16[8,32,2048]{2,1,0:T(8,128)(2,1)}, u32[]{:S(2)}, u32[]{:S(2)}) async-start(bf16[8,32,2048]{2,1,0:T(8,128)(2,1)} %bitcast.75), calls=%async_computation.3 | async-start | bytes 2097152 | tf_op jit(solution)/shard_map/all_to_all | solution.py:86
  271.5 2.2 copy-start.7
Sparse Core Ops, SparseCore 0:
  10.1 51.7 all-gather.2
  96.3 64.4 reduce-scatter.2
  164.3 31.4 all-gather.4
  233.9 29.6 all-reduce.2
  267.0 81.1 reduce-scatter.4
where the time goes:
time: 357 us
  waiting for transfers between devices  253 us (71%)
  matrix products  57.5 us (16%)
  starting transfers between devices  15.7 us (4%)
  between operations  14 us (4%)
  other arithmetic  12.2 us (3%)
  local copies, waits for them, and re-layouts  4.6 us (1%)
    reduce_scatter x1, waiting for transfers between devices, per_device(): lax.psum_scatter(partial_value.astype(jnp.bfloat16), 'tensor', scatter_di...  64.6 us
    all_gather x1, waiting for transfers between devices, per_device(): shard_rows = lax.all_gather(tokens, 'expert', axis=0, tiled=True)  54 us
    all_to_all x1, waiting for transfers between devices, per_device(): lax.all_to_all(expert_out.reshape(n_expert, per_peer, width_part), 'exper...  36.2 us
    reduce_scatter x1, waiting for transfers between devices, per_device(): lax.psum_scatter(jnp.dot(hidden_all, frozen_down_weight, preferred_elemen...  33.2 us
    all_to_all x1, waiting for transfers between devices, per_device(): lax.all_to_all(send_grads, 'expert', split_axis=0, concat_axis=0, tiled=T...  23.9 us
    all_to_all x1, waiting for transfers between devices, per_device(): lax.all_to_all(send_inputs, 'expert', split_axis=0, concat_axis=0, tiled=...  23.4 us
    psum x1, waiting for transfers between devices, per_device(): lax.psum(jnp.einsum('bcwk,cko->cbwo', incoming_input_rows, adapter_down_w...  16.4 us
    dot_general x1, matrix products, per_device(): jnp.dot(shard_rows, frozen_up_weight, preferred_element_type=jnp.float32)  14.9 us
  transfers between devices with their start and end apart: 8, of which 7 were waited for; matrix products, arithmetic and copies ran while one was open for 10% of the time, Pallas kernels for 0%

commit v1 on v0

--- a/solution.py
+++ b/solution.py
@@ -29,7 +29,14 @@
     most_slots = max(2, 4 * tok_count // all_experts)
     slot_total = all_experts * most_slots
     per_peer = expert_resident * most_slots
-    shard_rows = lax.all_gather(tokens, "expert", axis=0, tiled=True)
+    ring = [tokens]
+    for hop in range(7):
+        ring.append(lax.ppermute(ring[-1], "expert", [(dev, (dev + 1) % 8) for dev in range(8)]))
+    shard_rows = jnp.roll(
+        jnp.concatenate(ring[::-1], axis=0),
+        (lax.axis_index("expert") + 1) * ring[0].shape[0],
+        axis=0,
+    )
     gate_part = jnp.dot(shard_rows, frozen_gate_weight, preferred_element_type=jnp.float32)
     up_part = jnp.dot(shard_rows, frozen_up_weight, preferred_element_type=jnp.float32)
     partial_value = jnp.concatenate([gate_part, up_part], axis=1)

time: 357 us -> 372 us (1.042)
  waiting for transfers between devices: 253 us -> 262 us
  local copies, waits for them, and re-layouts: 4.6 us -> 12.2 us
  matrix products: 57.5 us -> 52 us
    ppermute x0 -> x7, waiting for transfers between devices: none -> 66 us  [per_device(): lax.ppermute(ring[-1], 'expert', [(dev, (dev + 1) % 8) for dev in range(8)])]
    all_gather x1 -> x0, waiting for transfers between devices: 54 us -> none  [per_device(): shard_rows = lax.all_gather(tokens, 'expert', axis=0, tiled=True)]
    unnamed x18 -> x41, local copies, waits for them, and re-layouts: 0.24 us -> 6.95 us
    dot_general x1, matrix products: 14.9 us -> 9.27 us  [per_device(): jnp.dot(shard_rows, frozen_up_weight, preferred_element_type=jnp.float32)]
  transfers between devices with their start and end apart: 8 -> 14, of which waited for: 7 -> 13; matrix products, arithmetic and copies ran while one was open for 10% -> 10% of each run, Pallas kernels for 0% -> 0%
where the time goes in v1:
time: 372 us; the launch traced here: 371 us
  waiting for transfers between devices  262 us (70%)
  matrix products  52 us (14%)
  starting transfers between devices  18.6 us (5%)
  between operations  14.1 us (4%)
  local copies, waits for them, and re-layouts  12.2 us (3%)
  other arithmetic  12.2 us (3%)
    ppermute x7, waiting for transfers between devices, per_device(): lax.ppermute(ring[-1], 'expert', [(dev, (dev + 1) % 8) for dev in range(8)])  66 us
    reduce_scatter x1, waiting for transfers between devices, per_device(): lax.psum_scatter(partial_value.astype(jnp.bfloat16), 'tensor', scatter_di...  63.1 us
    all_to_all x1, waiting for transfers between devices, per_device(): lax.all_to_all(expert_out.reshape(n_expert, per_peer, width_part), 'exper...  36.2 us
    reduce_scatter x1, waiting for transfers between devices, per_device(): lax.psum_scatter(jnp.dot(hidden_all, frozen_down_weight, preferred_elemen...  33 us
    all_to_all x1, waiting for transfers between devices, per_device(): lax.all_to_all(send_grads, 'expert', split_axis=0, concat_axis=0, tiled=T...  23.9 us
    all_to_all x1, waiting for transfers between devices, per_device(): lax.all_to_all(send_inputs, 'expert', split_axis=0, concat_axis=0, tiled=...  23.2 us
    psum x1, waiting for transfers between devices, per_device(): lax.psum(jnp.einsum('bcwk,cko->cbwo', incoming_input_rows, adapter_down_w...  16.7 us
    dot_general x1, matrix products, per_device(): jnp.dot(hidden_all, frozen_down_weight, preferred_element_type=jnp.float32)  13.1 us
  transfers between devices with their start and end apart: 14, of which 13 were waited for; matrix products, arithmetic and copies ran while one was open for 10% of the time, Pallas kernels for 0%

profile of v1, /device:TPU:0, one launch (start us, length us, event | category | flops | bytes accessed | tf_op | source)
XLA Modules:
  0.0 371.4 jit_solution(1128613157754428396)
XLA Ops:
  7.2 3.0 collective-permute-start
  10.3 9.6 %collective-permute-done = bf16[64,2048]{1,0:T(8,128)(2,1)S(1)} collective-permute-done((bf16[64,2048]{1,0:T(8,128)(2,1)}, bf16[64,2048]{1,0:T(8,128)(2,1)S(1)}, u32[]{:S(2)}, u32[]{:S(2)}) %collective-permute-start) | collective-permute-done | bytes 262176 | tf_op jit(solution)/shard_map/ppermute | solution.py:34
  19.8 10.2 %collective-permute-done.1 = bf16[64,2048]{1,0:T(8,128)(2,1)S(1)} collective-permute-done((bf16[64,2048]{1,0:T(8,128)(2,1)S(1)}, bf16[64,2048]{1,0:T(8,128)(2,1)S(1)}, u32[]{:S(2)}, u32[]{:S(2)}) %collective-permute-start.1) | collective-permute-done | bytes 262176 | tf_op jit(solution)/shard_map/ppermute | solution.py:34
  30.0 9.3 %collective-permute-done.2 = bf16[64,2048]{1,0:T(8,128)(2,1)S(1)} collective-permute-done((bf16[64,2048]{1,0:T(8,128)(2,1)S(1)}, bf16[64,2048]{1,0:T(8,128)(2,1)S(1)}, u32[]{:S(2)}, u32[]{:S(2)}) %collective-permute-start.2) | collective-permute-done | bytes 262176 | tf_op jit(solution)/shard_map/ppermute | solution.py:34
  39.3 9.1 %collective-permute-done.3 = bf16[64,2048]{1,0:T(8,128)(2,1)S(1)} collective-permute-done((bf16[64,2048]{1,0:T(8,128)(2,1)S(1)}, bf16[64,2048]{1,0:T(8,128)(2,1)S(1)}, u32[]{:S(2)}, u32[]{:S(2)}) %collective-permute-start.3) | collective-permute-done | bytes 262176 | tf_op jit(solution)/shard_map/ppermute | solution.py:34
  48.4 9.1 %collective-permute-done.4 = bf16[64,2048]{1,0:T(8,128)(2,1)S(1)} collective-permute-done((bf16[64,2048]{1,0:T(8,128)(2,1)S(1)}, bf16[64,2048]{1,0:T(8,128)(2,1)S(1)}, u32[]{:S(2)}, u32[]{:S(2)}) %collective-permute-start.4) | collective-permute-done | bytes 262176 | tf_op jit(solution)/shard_map/ppermute | solution.py:34
  57.4 0.7 copy-done.2
  58.1 9.5 %collective-permute-done.5 = bf16[64,2048]{1,0:T(8,128)(2,1)} collective-permute-done((bf16[64,2048]{1,0:T(8,128)(2,1)S(1)}, bf16[64,2048]{1,0:T(8,128)(2,1)}, u32[]{:S(2)}, u32[]{:S(2)}) %collective-permute-start.5) | collective-permute-done | bytes 262176 | tf_op jit(solution)/shard_map/ppermute | solution.py:34
  67.6 9.4 %collective-permute-done.6 = bf16[64,2048]{1,0:T(8,128)(2,1)} collective-permute-done((bf16[64,2048]{1,0:T(8,128)(2,1)}, bf16[64,2048]{1,0:T(8,128)(2,1)}, u32[]{:S(2)}, u32[]{:S(2)}) %collective-permute-start.6) | collective-permute-done | bytes 262176 | tf_op jit(solution)/shard_map/ppermute | solution.py:34
  77.0 1.0 constant_dynamic-update-slice_fusion.15
  78.0 1.0 constant_dynamic-update-slice_fusion.14
  78.9 1.0 constant_dynamic-update-slice_fusion.13
  80.0 1.0 constant_dynamic-update-slice_fusion.8
  81.0 1.0 constant_dynamic-update-slice_fusion.7
  82.0 1.0 constant_dynamic-update-slice_fusion.6
  83.2 12.5 %convolution_convert_fusion.1 = bf16[512,3584]{1,0:T(8,128)(2,1)} fusion(bf16[2048,3584]{1,0:T(8,128)(2,1)} %param.10, bf16[1024,2048]{1,0:T(8,128)(2,1)S(1)} %constant_dynamic-update-slice_fusion, s32[]{:T(128)S(6)} %select_n.14), kind=kOutput, calls=%fused_computation.2 | convolution fusion | flops 7518027776 | bytes 20447236 | tf_op jit(solution)/shard_map/dot_general | solution.py:40
  95.7 9.3 %convolution_convert_fusion = bf16[512,3584]{1,0:T(8,128)(2,1)} fusion(bf16[2048,3584]{1,0:T(8,128)(2,1)S(1)} %bitcast.77, bf16[1024,2048]{1,0:T(8,128)(2,1)S(1)} %constant_dynamic-update-slice_fusion, s32[]{:T(128)S(6)} %select_n.14), kind=kOutput, calls=%fused_computation.1 | convolution fusion | flops 7518027776 | bytes 20447236 | tf_op jit(solution)/shard_map/dot_general | solution.py:41
  104.9 6.9 %pad_maximum_fusion = bf16[512,7168]{1,0:T(8,128)(2,1)} fusion(bf16[512,3584]{1,0:T(8,128)(2,1)} %convolution_convert_fusion, bf16[512,3584]{1,0:T(8,128)(2,1)} %convolution_convert_fusion.1), kind=kLoop, calls=%fused_computation | loop fusion | flops 14680064 | bytes 14680064 | tf_op jit(solution)/shard_map/concatenate | solution.py:42
  111.9 63.1 %reduce-scatter.3.cloned.1.call-done = bf16[128,7168]{1,0:T(8,128)(2,1)} async-done(((bf16[512,7168]{1,0:T(8,128)(2,1)}), bf16[128,7168]{1,0:T(8,128)(2,1)}) %reduce-scatter.3.cloned.1.call-update) | async-done | bytes 1835024 | tf_op jit(solution)/shard_map/reduce_scatter | solution.py:43
  175.0 1.9 convert_element_type.72
  176.9 1.4 fusion.8
  178.5 0.1 reshape.81
  178.6 1.5 mul.82
  180.1 1.7 mul.83
  181.9 0.1 mul.80
  182.0 0.2 fusion.15
  182.2 2.7 convolution_convert_fusion.3
  184.9 5.5 %all-to-all-start.2 = ((bf16[8,32,2048]{2,1,0:T(8,128)(2,1)}), bf16[8,32,2048]{2,1,0:T(8,128)(2,1)S(1)}, u32[]{:S(2)}, u32[]{:S(2)}) async-start(bf16[8,32,2048]{2,1,0:T(8,128)(2,1)} %bitcast.75), calls=%async_computation.4 | async-start | bytes 2097152 | tf_op jit(solution)/shard_map/all_to_all | solution.py:109
  190.4 0.1 convert_element_type.79
  190.7 1.4 convolution_convert_fusion.5
  192.2 23.9 %all-to-all-done.2 = bf16[8,32,2048]{2,1,0:T(8,128)(2,1)S(1)} async-done(((bf16[8,32,2048]{2,1,0:T(8,128)(2,1)}), bf16[8,32,2048]{2,1,0:T(8,128)(2,1)S(1)}, u32[]{:S(2)}, u32[]{:S(2)}) %all-to-all-start.2) | async-done | bytes 1048608 | tf_op jit(solution)/shard_map/all_to_all | solution.py:109
  216.1 4.2 %all-to-all-start = ((bf16[8,32,2048]{2,1,0:T(8,128)(2,1)}), bf16[8,32,2048]{2,1,0:T(8,128)(2,1)}, u32[]{:S(2)}, u32[]{:S(2)}) async-start(bf16[8,32,2048]{2,1,0:T(8,128)(2,1)} %bitcast.74), calls=%async_computation.2 | async-start | bytes 2097152 | tf_op jit(solution)/shard_map/all_to_all | solution.py:75
  220.3 0.2 all-reduce.3.cloned.1.call-start
  220.5 0.6 copy.46
  221.1 1.5 fusion.9
  222.6 23.2 %all-to-all-done = bf16[8,32,2048]{2,1,0:T(8,128)(2,1)} async-done(((bf16[8,32,2048]{2,1,0:T(8,128)(2,1)}), bf16[8,32,2048]{2,1,0:T(8,128)(2,1)}, u32[]{:S(2)}, u32[]{:S(2)}) %all-to-all-start) | async-done | bytes 1048608 | tf_op jit(solution)/shard_map/all_to_all | solution.py:75
  245.8 3.0 fusion.12
  249.0 13.1 %convolution_convert_fusion.2 = bf16[512,2048]{1,0:T(8,128)(2,1)} fusion(bf16[512,3584]{1,0:T(8,128)(2,1)} %all-gather.2.cloned.1.call-done, bf16[3584,2048]{1,0:T(8,128)(2,1)} %param.12), kind=kOutput, calls=%fused_computation.5 | convolution fusion | flops 7517241344 | bytes 20447232 | tf_op jit(solution)/shard_map/dot_general | solution.py:48
  262.1 16.7 %all-reduce.3.cloned.1.call-done = (bf16[4,8,8,128]{3,2,1,0:T(8,128)(2,1)}, bf16[4,8,8,128]{3,1,2,0:T(8,128)(2,1)}) async-done(((bf16[4,8,8,128]{3,2,1,0:T(8,128)(2,1)}, bf16[4,8,8,128]{3,1,2,0:T(8,128)(2,1)}), (bf16[4,8,8,128]{3,2,1,0:T(8,128)(2,1)}, bf16[4,8,8,128]{3,1,2,0:T(8,128)(2,1)})) %all-reduce.3.cloned.1.call-update) | async-done | bytes 131088 | tf_op jit(solution)/shard_map/psum | solution.py:81
  278.7 1.3 fusion
  280.1 1.0 copy.62
  281.1 5.5 %all-to-all-start.1 = ((bf16[8,32,2048]{2,1,0:T(8,128)(2,1)}), bf16[8,32,2048]{2,1,0:T(8,128)(2,1)}, u32[]{:S(2)}, u32[]{:S(2)}) async-start(bf16[8,32,2048]{2,1,0:T(8,128)(2,1)} %bitcast.73), calls=%async_computation.3 | async-start | bytes 2097152 | tf_op jit(solution)/shard_map/all_to_all | solution.py:93
  286.8 2.1 bitcast_convert_fusion
  288.8 3.5 bitcast_convert_fusion.1
  292.3 36.2 %all-to-all-done.1 = bf16[8,32,2048]{2,1,0:T(8,128)(2,1)} async-done(((bf16[8,32,2048]{2,1,0:T(8,128)(2,1)}), bf16[8,32,2048]{2,1,0:T(8,128)(2,1)}, u32[]{:S(2)}, u32[]{:S(2)}) %all-to-all-start.1) | async-done | bytes 1048608 | tf_op jit(solution)/shard_map/all_to_all | solution.py:93
  328.5 1.5 fusion.25
  330.0 33.0 %reduce-scatter.5.cloned.1.call-done = bf16[64,2048]{1,0:T(8,128)(2,1)} async-done(((bf16[512,2048]{1,0:T(8,128)(2,1)}), bf16[64,2048]{1,0:T(8,128)(2,1)}) %reduce-scatter.5.cloned.1.call-update) | async-done | bytes 262160 | tf_op jit(solution)/shard_map/reduce_scatter | solution.py:47
  363.1 1.8 fusion.21
  (58 shorter events, 1.0 us)
Async XLA Ops:
  7.2 214.0 %copy-start = (bf16[4,128,2048]{2,1,0:T(8,128)(2,1)S(1)}, bf16[4,128,2048]{2,1,0:T(8,128)(2,1)}, u32[]{:S(2)}) copy-start(bf16[4,128,2048]{2,1,0:T(8,128)(2,1)} %param.14) | copy-start | bytes 6291460
  7.2 75.9 %copy-start.1 = (bf16[64,2048]{1,0:T(8,128)(2,1)S(1)}, bf16[64,2048]{1,0:T(8,128)(2,1)}, u32[]{:S(2)}) copy-start(bf16[64,2048]{1,0:T(8,128)(2,1)} %param.9) | copy-start | bytes 786436
  7.2 167.8 %reduce-scatter.3.cloned.1.call-start = ((), (), s32[]{:S(2)}) async-start(), calls=%async_computation.5 | async-start | bytes 9175040 | tf_op jit(solution)/shard_map/reduce_scatter | solution.py:43
  7.2 12.6 %collective-permute-start = (bf16[64,2048]{1,0:T(8,128)(2,1)}, bf16[64,2048]{1,0:T(8,128)(2,1)S(1)}, u32[]{:S(2)}, u32[]{:S(2)}) collective-permute-start(bf16[64,2048]{1,0:T(8,128)(2,1)} %param.9), channel_id=1, source_target_pairs={{0,4},{4,8},{8,12},{12,16},{16,20},{20,24},{24,28},{28,0},{1,5},{5... | collective-permute-start | bytes 786440 | tf_op jit(solution)/shard_map/ppermute | solution.py:34
  19.8 10.2 %collective-permute-start.1 = (bf16[64,2048]{1,0:T(8,128)(2,1)S(1)}, bf16[64,2048]{1,0:T(8,128)(2,1)S(1)}, u32[]{:S(2)}, u32[]{:S(2)}) collective-permute-start(bf16[64,2048]{1,0:T(8,128)(2,1)S(1)} %collective-permute-done), channel_id=1, source_target_pairs={{0,4},{4,8},{8,12},{12,16},{16,20},{20,24},{24,28},{28,0},{1,5},{5... | collective-permute-start | bytes 786440 | tf_op jit(solution)/shard_map/ppermute | solution.py:34
  30.0 9.3 %collective-permute-start.2 = (bf16[64,2048]{1,0:T(8,128)(2,1)S(1)}, bf16[64,2048]{1,0:T(8,128)(2,1)S(1)}, u32[]{:S(2)}, u32[]{:S(2)}) collective-permute-start(bf16[64,2048]{1,0:T(8,128)(2,1)S(1)} %collective-permute-done.1), channel_id=1, source_target_pairs={{0,4},{4,8},{8,12},{12,16},{16,20},{20,24},{24,28},{28,0},{1,5},{5... | collective-permute-start | bytes 786440 | tf_op jit(solution)/shard_map/ppermute | solution.py:34
  39.3 9.1 %collective-permute-start.3 = (bf16[64,2048]{1,0:T(8,128)(2,1)S(1)}, bf16[64,2048]{1,0:T(8,128)(2,1)S(1)}, u32[]{:S(2)}, u32[]{:S(2)}) collective-permute-start(bf16[64,2048]{1,0:T(8,128)(2,1)S(1)} %collective-permute-done.2), channel_id=1, source_target_pairs={{0,4},{4,8},{8,12},{12,16},{16,20},{20,24},{24,28},{28,0},{1,5},{5... | collective-permute-start | bytes 786440 | tf_op jit(solution)/shard_map/ppermute | solution.py:34
  48.4 9.1 %collective-permute-start.4 = (bf16[64,2048]{1,0:T(8,128)(2,1)S(1)}, bf16[64,2048]{1,0:T(8,128)(2,1)S(1)}, u32[]{:S(2)}, u32[]{:S(2)}) collective-permute-start(bf16[64,2048]{1,0:T(8,128)(2,1)S(1)} %collective-permute-done.3), channel_id=1, source_target_pairs={{0,4},{4,8},{8,12},{12,16},{16,20},{20,24},{24,28},{28,0},{1,5},{5... | collective-permute-start | bytes 786440 | tf_op jit(solution)/shard_map/ppermute | solution.py:34
  57.4 0.7 copy-start.2
  58.1 9.5 %collective-permute-start.5 = (bf16[64,2048]{1,0:T(8,128)(2,1)S(1)}, bf16[64,2048]{1,0:T(8,128)(2,1)}, u32[]{:S(2)}, u32[]{:S(2)}) collective-permute-start(bf16[64,2048]{1,0:T(8,128)(2,1)S(1)} %collective-permute-done.4), channel_id=1, source_target_pairs={{0,4},{4,8},{8,12},{12,16},{16,20},{20,24},{24,28},{28,0},{1,5},{5... | collective-permute-start | bytes 786440 | tf_op jit(solution)/shard_map/ppermute | solution.py:34
  67.6 9.4 %collective-permute-start.6 = (bf16[64,2048]{1,0:T(8,128)(2,1)}, bf16[64,2048]{1,0:T(8,128)(2,1)}, u32[]{:S(2)}, u32[]{:S(2)}) collective-permute-start(bf16[64,2048]{1,0:T(8,128)(2,1)} %collective-permute-done.5), channel_id=1, source_target_pairs={{0,4},{4,8},{8,12},{12,16},{16,20},{20,24},{24,28},{28,0},{1,5},{5... | collective-permute-start | bytes 786440 | tf_op jit(solution)/shard_map/ppermute | solution.py:34
  67.6 15.3 %copy-start.3 = (bf16[64,2048]{1,0:T(8,128)(2,1)S(1)}, bf16[64,2048]{1,0:T(8,128)(2,1)}, u32[]{:S(2)}) copy-start(bf16[64,2048]{1,0:T(8,128)(2,1)} %copy-done.2) | copy-start | bytes 786436
  83.0 12.6 %slice-start = ((s8[14680064]{0:T(1024)(128)(4,1)}), s8[4194304]{0:T(1024)(128)(4,1)S(1)}, s32[]{:S(2)}) async-start(s8[14680064]{0:T(1024)(128)(4,1)} %bitcast.76), calls=%async_computation.9 | async-start | bytes 8388608
  83.1 12.5 %slice-start.1 = ((s8[14680064]{0:T(1024)(128)(4,1)}), s8[4194304]{0:T(1024)(128)(4,1)S(1)}, s32[]{:S(2)}) async-start(s8[14680064]{0:T(1024)(128)(4,1)} %bitcast.76), calls=%async_computation.10 | async-start | bytes 8388608
  83.1 12.5 %slice-start.2 = ((s8[14680064]{0:T(1024)(128)(4,1)}), s8[4194304]{0:T(1024)(128)(4,1)S(1)}, s32[]{:S(2)}) async-start(s8[14680064]{0:T(1024)(128)(4,1)} %bitcast.76), calls=%async_computation.11 | async-start | bytes 8388608
  83.2 12.5 %slice-start.3 = ((s8[14680064]{0:T(1024)(128)(4,1)}), s8[2097152]{0:T(1024)(128)(4,1)S(1)}, s32[]{:S(2)}) async-start(s8[14680064]{0:T(1024)(128)(4,1)} %bitcast.76), calls=%async_computation.12 | async-start | bytes 4194304
  111.8 66.5 %copy-start.5 = (s32[64,2]{0,1:T(2,128)S(1)}, s32[64,2]{0,1:T(2,128)}, u32[]{:S(2)}) copy-start(s32[64,2]{0,1:T(2,128)} %param.15) | copy-start | bytes 1540
  111.8 137.1 %all-gather.2.cloned.1.call-start = ((), (), s32[]{:S(2)}) async-start(), calls=%async_computation.6 | async-start | bytes 4587520 | tf_op jit(solution)/shard_map/all_gather | solution.py:46
  176.9 4.9 %copy-start.6 = (f32[64,2]{0,1:T(2,128)S(1)}, f32[64,2]{0,1:T(2,128)}, u32[]{:S(2)}) copy-start(f32[64,2]{0,1:T(2,128)} %param.16) | copy-start | bytes 1540
  184.9 31.2 %all-to-all-start.2 = ((bf16[8,32,2048]{2,1,0:T(8,128)(2,1)}), bf16[8,32,2048]{2,1,0:T(8,128)(2,1)S(1)}, u32[]{:S(2)}, u32[]{:S(2)}) async-start(bf16[8,32,2048]{2,1,0:T(8,128)(2,1)} %bitcast.75), calls=%async_computation.4 | async-start | bytes 2097152 | tf_op jit(solution)/shard_map/all_to_all | solution.py:109
  216.1 29.8 %all-to-all-start = ((bf16[8,32,2048]{2,1,0:T(8,128)(2,1)}), bf16[8,32,2048]{2,1,0:T(8,128)(2,1)}, u32[]{:S(2)}, u32[]{:S(2)}) async-start(bf16[8,32,2048]{2,1,0:T(8,128)(2,1)} %bitcast.74), calls=%async_computation.2 | async-start | bytes 2097152 | tf_op jit(solution)/shard_map/all_to_all | solution.py:75
  220.3 58.4 %all-reduce.3.cloned.1.call-start = ((), (), s32[]{:S(2)}) async-start(), calls=%async_computation.8 | async-start | bytes 262144 | tf_op jit(solution)/shard_map/psum | solution.py:81
  248.9 114.2 %reduce-scatter.5.cloned.1.call-start = ((), (), s32[]{:S(2)}) async-start(), calls=%async_computation.7 | async-start | bytes 2359296 | tf_op jit(solution)/shard_map/reduce_scatter | solution.py:47
  278.7 8.0 %copy-start.4 = (bf16[4,8,8,128]{3,2,1,0:T(8,128)(2,1)S(1)}, bf16[4,8,8,128]{3,2,1,0:T(8,128)(2,1)}, u32[]{:S(2)}) copy-start(bf16[4,8,8,128]{3,2,1,0:T(8,128)(2,1)} %get-tuple-element.3) | copy-start | bytes 196612
  280.1 8.8 %copy-start.7 = (bf16[4,8,8,128]{3,1,2,0:T(8,128)(2,1)S(1)}, bf16[4,8,8,128]{3,1,2,0:T(8,128)(2,1)}, u32[]{:S(2)}) copy-start(bf16[4,8,8,128]{3,1,2,0:T(8,128)(2,1)} %get-tuple-element.4) | copy-start | bytes 196612
  281.1 47.4 %all-to-all-start.1 = ((bf16[8,32,2048]{2,1,0:T(8,128)(2,1)}), bf16[8,32,2048]{2,1,0:T(8,128)(2,1)}, u32[]{:S(2)}, u32[]{:S(2)}) async-start(bf16[8,32,2048]{2,1,0:T(8,128)(2,1)} %bitcast.73), calls=%async_computation.3 | async-start | bytes 2097152 | tf_op jit(solution)/shard_map/all_to_all | solution.py:93
Sparse Core Ops, SparseCore 0:
  111.9 63.0 reduce-scatter.2
  178.5 31.4 all-gather.1
  249.0 29.6 all-reduce.2
  282.1 80.9 reduce-scatter.4
